TPU v7x, 256 devices: a whole 4x4x8 slice. The times are simulated.
256 devices in a mesh: det: 64 (over x, z, core), row: 4 (over y).
Axes of the slice: x: 4, y: 4, z: 8, core: 2. Of those that a mesh axis runs over, the one named last changes fastest.
Arguments:
- images: bfloat16 [384, 3, 384, 384], P('det', None, 'row'), may hold values from -6 to 6
- warp_rows: bfloat16 [384, 3, 384, 384], P('det', None, 'row'), may hold values from -0.3125 to 0.3125
- warp_cols: bfloat16 [384, 3, 384, 384], P('det'), may hold values from -0.3125 to 0.3125
- psf_coef: float32 [384, 3, 21], P('det'), may hold values from -1.25 to 1.25
- taps: float32 [21, 21], replicated, may hold values from -1.25 to 1.25
- dest_patch: int32 [3456, 1], replicated, may hold values from 0 to 63; in each aligned block of 54 rows (0 to 53, 54 to 107, ...) at most 2 rows name the same one
- dest_block: int32 [3456], replicated, may hold values from 0 to 2
- weight_index: int32 [384, 3], replicated, may hold values from 0 to 7
- weight_table: float32 [8], replicated, may hold values from 0.25 to 4
- patch_home: int32 [64], replicated, may hold values from 0 to 63, each once
Outputs:
- difference: bfloat16 [384, 3, 384, 384], P('det', None, 'row')
- coadd: bfloat16 [64, 384, 384], P('det', 'row')
Inputs may be any that keep to these rules, and one draw needn't show every extreme that they name: `dest_patch`: within the 54 rows of one device (an aligned block of rows), no patch is named more than 2 times. `patch_home`: each position once.
All inputs are finite; a program needn't handle non-finite values.
Results may differ from a plain program's by a relative error of at most 0.0082.
Values may be sent and summed in bfloat16 or wider, within the bound.
A program may use at most 128 MiB of HBM per device.

v0:
```python
import jax
import jax.numpy as jnp
from jax import lax
from jax.sharding import PartitionSpec as P

TILE = 128


def extended(value, sides, width):
    for axis, dim in sides:
        size, length = (lax.axis_size(axis), value.shape[dim])
        up = [(i, (i + 1) % size) for i in range(size - 1)]
        down = [(j, i) for i, j in up]
        last = lax.slice_in_dim(value, length - width, length, axis=dim)
        first = lax.slice_in_dim(value, 0, width, axis=dim)
        before = lax.ppermute(last, axis, up)
        after = lax.ppermute(first, axis, down)
        value = jnp.concatenate([before, value, after], axis=dim)
    return value


def toeplitz_table(values, out_len, in_len):
    span_len = values.shape[1]
    offsets = jnp.arange(in_len)[None, :] - jnp.arange(out_len)[:, None]
    picks = (offsets[:, :, None] == jnp.arange(span_len)[None, None, :]).astype(jnp.float32)
    return jnp.einsum("oij,kj->koi", picks, values.astype(jnp.float32)).astype(jnp.bfloat16)


def per_device(
    images,
    warp_rows,
    warp_cols,
    psf_coef,
    taps,
    dest_patch,
    dest_block,
    weight_index,
    weight_table,
    patch_home,
):
    det_count, visit_count, band_rows, side_cols = images.shape
    kernel_count, tap_count = taps.shape
    reach = (tap_count - 1) // 2
    tile_cols = TILE
    tile_count = side_cols // tile_cols
    det_devices = lax.axis_size("det")
    my_index = lax.axis_index("det")
    image_count = det_count * visit_count
    piece_count = image_count * tile_count
    capacity = max(2, 2 * ((piece_count + det_devices - 1) // det_devices))
    slot_count = det_devices * capacity
    padded_rows = band_rows + 2 * reach
    col_warped = jnp.einsum(
        "dvbs,dvst->dvbt", images, warp_cols, preferred_element_type=jnp.float32
    ).astype(jnp.bfloat16)
    warped = jnp.einsum(
        "dvbr,dvrs->dvbs",
        warp_rows,
        lax.all_gather(col_warped, "row", axis=2, tiled=True),
        preferred_element_type=jnp.float32,
    ).astype(jnp.bfloat16)
    padded = extended(warped, (("row", 2),), reach)
    taps_half = taps.astype(jnp.bfloat16)
    col_table = toeplitz_table(taps_half, tile_cols, tile_cols + 2 * reach)
    tiles_in = padded.reshape(image_count, padded_rows, side_cols)
    coef_rows = psf_coef.reshape(image_count, kernel_count)

    def match_image(inputs):
        tile_image, coef_row = inputs
        widened = jnp.pad(tile_image, ((0, 0), (reach, reach)))
        windows = jnp.stack(
            [
                widened[
                    :, column_tile * tile_cols : column_tile * tile_cols + tile_cols + 2 * reach
                ]
                for column_tile in range(tile_count)
            ],
            axis=1,
        )
        conv_cols = jnp.einsum(
            "rtw,kcw->krtc", windows, col_table, preferred_element_type=jnp.float32
        ).astype(jnp.bfloat16)
        conv_cols = conv_cols.reshape(kernel_count, padded_rows, side_cols)
        scaled = (coef_row[:, None] * taps).astype(jnp.bfloat16)
        row_table = toeplitz_table(scaled, band_rows, padded_rows)
        return jnp.einsum("kbr,krs->bs", row_table, conv_cols, preferred_element_type=jnp.float32)

    matched = lax.map(match_image, (tiles_in, coef_rows))
    level_count = weight_table.shape[0]
    level_onehot = (weight_index[:, :, None] == jnp.arange(level_count)[None, None, :]).astype(
        jnp.float32
    )
    weight_all = jnp.sum(level_onehot * weight_table[None, None, :], axis=2)
    weight_mine = lax.dynamic_slice_in_dim(weight_all, my_index * det_count, det_count, 0).reshape(
        image_count
    )
    weighted = (
        (weight_mine[:, None, None] * matched)
        .astype(jnp.bfloat16)
        .reshape(image_count, band_rows, tile_count, tile_cols)
    )
    patch_count = patch_home.shape[0]
    patch_ids = dest_patch[:, 0]
    owner_all = jnp.sum(
        jnp.where(patch_ids[:, None] == jnp.arange(patch_count)[None, :], patch_home[None, :], 0),
        axis=1,
    )
    owner_grid = owner_all.reshape(det_devices, piece_count)
    earlier = jnp.arange(piece_count)[None, :] < jnp.arange(piece_count)[:, None]
    rank_grid = jnp.sum(
        ((owner_grid[:, :, None] == owner_grid[:, None, :]) & earlier[None]).astype(jnp.int32),
        axis=2,
    )
    slot_grid = owner_grid * capacity + rank_grid
    slot_mine = lax.dynamic_slice_in_dim(slot_grid, my_index, 1, 0)[0]
    send_pick = (
        (jnp.arange(slot_count)[:, None] == slot_mine[None, :])
        .astype(jnp.bfloat16)
        .reshape(slot_count, image_count, tile_count)
    )
    weight_pieces = jnp.repeat(weight_all.reshape(-1), tile_count)
    to_mine = owner_all == my_index
    block_onehot = (dest_block[:, None] == jnp.arange(tile_count)[None, :]).astype(jnp.float32)
    denominator = jnp.sum(
        jnp.where(to_mine[:, None], block_onehot * weight_pieces[:, None], 0.0), axis=0
    )
    source_slot = jnp.arange(
        det_devices * piece_count
    ) // piece_count * capacity + rank_grid.reshape(-1)
    slot_onehot = (
        (source_slot[:, None] == jnp.arange(slot_count)[None, :]) & to_mine[:, None]
    ).astype(jnp.float32)
    gather_matrix = jnp.einsum("iq,is->qs", block_onehot, slot_onehot).astype(jnp.bfloat16)
    outgoing = jnp.einsum(
        "spq,pbqc->sbc", send_pick, weighted, preferred_element_type=jnp.float32
    ).astype(jnp.bfloat16)
    received = lax.all_to_all(outgoing, "det", split_axis=0, concat_axis=0, tiled=True)
    numerator = jnp.einsum(
        "qs,sbc->bqc", gather_matrix, received, preferred_element_type=jnp.float32
    )
    template = (numerator / jnp.maximum(denominator, 1.0)[None, :, None]).astype(jnp.bfloat16)
    coadd_band = template.reshape(1, band_rows, side_cols)
    returned = jnp.einsum(
        "qs,bqc->sbc", gather_matrix, template, preferred_element_type=jnp.float32
    ).astype(jnp.bfloat16)
    arrived = lax.all_to_all(returned, "det", split_axis=0, concat_axis=0, tiled=True)
    local_template = jnp.einsum(
        "spq,sbc->pbqc", send_pick, arrived, preferred_element_type=jnp.float32
    )
    difference = (
        matched.reshape(image_count, band_rows, tile_count, tile_cols) - local_template
    ).astype(jnp.bfloat16)
    difference = difference.reshape(det_count, visit_count, band_rows, side_cols)
    return (difference, coadd_band)


def solution(mesh):
    placed = (
        P("det", None, "row", None),
        P("det", None, "row", None),
        P("det", None, None, None),
        P("det", None, None),
        P(),
        P(),
        P(),
        P(),
        P(),
        P(),
    )
    return jax.shard_map(
        per_device,
        mesh=mesh,
        in_specs=placed,
        out_specs=(P("det", None, "row", None), P("det", "row", None)),
        check_vma=False,
    )
```

profile of v0, /device:TPU:1, one launch (start us, length us, event | category | flops | bytes accessed | tf_op | source)
XLA Modules:
  0.0 490.7 jit_solution(14183806398760456192)
XLA Ops:
  8.5 4.7 convolution_convert_fusion.3
  15.2 62.1 %all-gather.2.cloned.1.call-done = bf16[6,3,384,384]{3,2,1,0:T(8,128)(2,1)} async-done(((bf16[6,3,96,384]{3,2,1,0:T(8,128)(2,1)}), bf16[6,3,384,384]{3,2,1,0:T(8,128)(2,1)}) %all-gather.2.cloned.1.call-update) | async-done | bytes 5308432 | tf_op jit(solution)/shard_map/all_gather | solution.py:59
  77.3 3.6 fusion.26
  87.8 3.8 collective-permute-done.1
  93.4 198.1 %while.12 = (s32[]{:T(128)}, f32[18,96,384]{2,1,0:T(8,128)}, f32[18,21]{1,0:T(8,128)S(1)}, f32[21,21]{1,0:T(8,128)S(1)}, bf16[18,116,384]{2,1,0:T(8,128)(2,1)}, /*index=5*/bf16[21,128,148]{1,2,0:T(8,128)(2,1)}, s32[]{:T(128)}) while((s32[]{:T(128)}, f32[18,96,384]{2,1,0:T(8,128)}, f32[18,21]{1,0:T(8,128)S(1)}, f32[21,21]{1,0:T(8,128)S(1)}, ...), condition=%wide.region_1.2_spmd, body=%wide.region_0.1_spmd.sunk | while | flops 468033056 | bytes 10274817 | solution.py:88
  95.7 3.2 convert_bitcast_fusion.2
  106.7 3.2 convert_bitcast_fusion.2
  117.7 3.2 convert_bitcast_fusion.2
  128.7 3.2 convert_bitcast_fusion.2
  139.7 3.2 convert_bitcast_fusion.2
  150.7 3.2 convert_bitcast_fusion.2
  161.7 3.2 convert_bitcast_fusion.2
  172.7 3.2 convert_bitcast_fusion.2
  183.7 3.2 convert_bitcast_fusion.2
  194.7 3.2 convert_bitcast_fusion.2
  205.7 3.2 convert_bitcast_fusion.2
  216.7 3.2 convert_bitcast_fusion.2
  227.7 3.2 convert_bitcast_fusion.2
  238.7 3.2 convert_bitcast_fusion.2
  249.7 3.2 convert_bitcast_fusion.2
  260.7 3.2 convert_bitcast_fusion.2
  271.7 3.2 convert_bitcast_fusion.2
  282.7 3.2 convert_bitcast_fusion.2
  291.5 3.1 multiply_convert_fusion.1
  294.5 3.6 reshape.134
  300.1 3.7 copy.71
  303.8 12.1 %all-to-all-start = ((bf16[128,96,128]{2,1,0:T(8,128)(2,1)}), bf16[128,96,128]{2,1,0:T(8,128)(2,1)}, u32[]{:S(2)}, u32[]{:S(2)}) async-start(bf16[128,96,128]{2,1,0:T(8,128)(2,1)} %copy.71), calls=%async_computation | async-start | bytes 6291456 | tf_op jit(solution)/shard_map/all_to_all | solution.py:137
  318.4 71.0 %all-to-all-done = bf16[128,96,128]{2,1,0:T(8,128)(2,1)} async-done(((bf16[128,96,128]{2,1,0:T(8,128)(2,1)}), bf16[128,96,128]{2,1,0:T(8,128)(2,1)}, u32[]{:S(2)}, u32[]{:S(2)}) %all-to-all-start) | async-done | bytes 3145760 | tf_op jit(solution)/shard_map/all_to_all | solution.py:137
  393.3 3.7 copy.74
  397.0 6.2 %all-to-all-start.1 = ((bf16[128,96,128]{2,1,0:T(8,128)(2,1)}), bf16[128,96,128]{2,1,0:T(8,128)(2,1)}, u32[]{:S(2)}, u32[]{:S(2)}) async-start(bf16[128,96,128]{2,1,0:T(8,128)(2,1)} %copy.74), calls=%async_computation.1 | async-start | bytes 6291456 | tf_op jit(solution)/shard_map/all_to_all | solution.py:146
  403.9 72.7 %all-to-all-done.1 = bf16[128,96,128]{2,1,0:T(8,128)(2,1)} async-done(((bf16[128,96,128]{2,1,0:T(8,128)(2,1)}), bf16[128,96,128]{2,1,0:T(8,128)(2,1)}, u32[]{:S(2)}, u32[]{:S(2)}) %all-to-all-start.1) | async-done | bytes 3145760 | tf_op jit(solution)/shard_map/all_to_all | solution.py:146
  476.7 3.3 fusion.15
  (207 shorter events, 164.6 us)
Async XLA Ops:
  7.2 1.3 copy-start
  7.2 6.1 %copy-start.9 = (f32[8]{0:T(128)S(1)}, f32[8]{0:T(128)}, u32[]{:S(2)}) copy-start(f32[8]{0:T(128)} %param.20) | copy-start | bytes 100
  7.2 6.1 %copy-start.7 = (s32[384,3]{0,1:T(4,128)S(1)}, s32[384,3]{0,1:T(4,128)}, u32[]{:S(2)}) copy-start(s32[384,3]{0,1:T(4,128)} %param.19) | copy-start | bytes 13828
  7.2 6.4 %copy-start.6 = (f32[6,3,21]{2,1,0:T(4,128)S(1)}, f32[6,3,21]{2,1,0:T(4,128)}, u32[]{:S(2)}) copy-start(f32[6,3,21]{2,1,0:T(4,128)} %param.15) | copy-start | bytes 4540
  7.2 6.4 %copy-start.5 = (s32[3456,1]{0,1:T(1,128)S(1)}, s32[3456,1]{0,1:T(1,128)}, u32[]{:S(2)}) copy-start(s32[3456,1]{0,1:T(1,128)} %param.17) | copy-start | bytes 41476
  7.2 6.5 %copy-start.8 = (s32[64]{0:T(128)S(1)}, s32[64]{0:T(128)}, u32[]{:S(2)}) copy-start(s32[64]{0:T(128)} %param.21) | copy-start | bytes 772
  7.2 70.1 %all-gather.2.cloned.1.call-start = ((), (), s32[]{:S(2)}) async-start(), calls=%async_computation.2 | async-start | bytes 6635520 | tf_op jit(solution)/shard_map/all_gather | solution.py:59
  13.2 64.1 %copy-start.2 = (bf16[6,3,96,384]{3,2,1,0:T(8,128)(2,1)S(1)}, bf16[6,3,96,384]{3,2,1,0:T(8,128)(2,1)}, u32[]{:S(2)}) copy-start(bf16[6,3,96,384]{3,2,1,0:T(8,128)(2,1)} %param.13) | copy-start | bytes 3981316
  15.2 69.8 %copy-start.3 = (f32[21,21]{1,0:T(8,128)S(1)}, f32[21,21]{1,0:T(8,128)}, u32[]{:S(2)}) copy-start(f32[21,21]{1,0:T(8,128)} %param.16) | copy-start | bytes 5296
  81.0 6.7 %collective-permute-start = (bf16[6,3,10,384]{3,2,1,0:T(8,128)(2,1)S(1)}, bf16[6,3,10,384]{3,2,1,0:T(8,128)(2,1)S(1)}, u32[]{:S(2)}, u32[]{:S(2)}) collective-permute-start(bf16[6,3,10,384]{3,2,1,0:T(8,128)(2,1)S(1)} %get-tuple-element.125), channel_id=1, source_target_pairs={{0,1},{1,2},{2,3},{4,5},{5,6},{6,7},{8,9},{9,10},{10,11},{12,13},{... | collective-permute-start | bytes 414728 | tf_op jit(solution)/shard_map/ppermute | solution.py:16
  83.7 7.9 %collective-permute-start.1 = (bf16[6,3,10,384]{3,2,1,0:T(8,128)(2,1)S(1)}, bf16[6,3,10,384]{3,2,1,0:T(8,128)(2,1)S(1)}, u32[]{:S(2)}, u32[]{:S(2)}) collective-permute-start(bf16[6,3,10,384]{3,2,1,0:T(8,128)(2,1)S(1)} %get-tuple-element.126), channel_id=1, source_target_pairs={{1,0},{2,1},{3,2},{5,4},{6,5},{7,6},{9,8},{10,9},{11,10},{13,12},{... | collective-permute-start | bytes 414728 | tf_op jit(solution)/shard_map/ppermute | solution.py:17
  303.8 13.3 %copy-start.4 = (s32[3456]{0:T(1024)S(1)}, s32[3456]{0:T(1024)}, u32[]{:S(2)}) copy-start(s32[3456]{0:T(1024)} %param.18) | copy-start | bytes 41476
  303.8 85.6 %all-to-all-start = ((bf16[128,96,128]{2,1,0:T(8,128)(2,1)}), bf16[128,96,128]{2,1,0:T(8,128)(2,1)}, u32[]{:S(2)}, u32[]{:S(2)}) async-start(bf16[128,96,128]{2,1,0:T(8,128)(2,1)} %copy.71), calls=%async_computation | async-start | bytes 6291456 | tf_op jit(solution)/shard_map/all_to_all | solution.py:137
  397.0 79.7 %all-to-all-start.1 = ((bf16[128,96,128]{2,1,0:T(8,128)(2,1)}), bf16[128,96,128]{2,1,0:T(8,128)(2,1)}, u32[]{:S(2)}, u32[]{:S(2)}) async-start(bf16[128,96,128]{2,1,0:T(8,128)(2,1)} %copy.74), calls=%async_computation.1 | async-start | bytes 6291456 | tf_op jit(solution)/shard_map/all_to_all | solution.py:146
  476.7 3.3 copy-start.1
Sparse Core Ops, SparseCore 0:
  13.4 63.8 all-gather.1
where the time goes:
time: 495 us; the launch traced here: 491 us
  waiting for transfers between devices  211 us (43%)
  matrix products  143 us (29%)
  local copies, waits for them, and re-layouts  92.9 us (19%)
  starting transfers between devices  22.4 us (5%)
  between operations  14.4 us (3%)
  other arithmetic  7.01 us (1%)
    all_to_all x1, waiting for transfers between devices, per_device(): lax.all_to_all(returned, 'det', split_axis=0, concat_axis=0, tiled=True)  72.7 us
    all_to_all x1, waiting for transfers between devices, per_device(): lax.all_to_all(outgoing, 'det', split_axis=0, concat_axis=0, tiled=True)  71 us
    all_gather x1, waiting for transfers between devices, per_device(): lax.all_gather(col_warped, 'row', axis=2, tiled=True)  62.1 us
    dot_general x18, matrix products, match_image(): jnp.einsum('rtw,kcw->krtc', windows, col_table, preferred_element_type=jn...  57.4 us
    convert_element_type x18, local copies, waits for them, and re-layouts, match_image(): conv_cols = jnp.einsum('rtw,kcw->krtc', windows, col_table, preferred_ele...  54.3 us
    dot_general x18, matrix products, match_image(): jnp.einsum('kbr,krs->bs', row_table, conv_cols, preferred_element_type=jn...  44.7 us
    dot_general x19, matrix products, toeplitz_table(): jnp.einsum('oij,kj->koi', picks, values.astype(jnp.float32))  22.1 us
    dynamic_slice x36, local copies, waits for them, and re-layouts, per_device(): matched = lax.map(match_image, (tiles_in, coef_rows))  18.7 us
  transfers between devices with their start and end apart: 5, of which 5 were waited for; matrix products, arithmetic and copies ran while one was open for 1% of the time, Pallas kernels for 0%

commit v1 on v0

--- a/solution.py
+++ b/solution.py
@@ -56,7 +56,9 @@
     warped = jnp.einsum(
         "dvbr,dvrs->dvbs",
         warp_rows,
-        lax.all_gather(col_warped, "row", axis=2, tiled=True),
+        jnp.concatenate(
+            lax.all_to_all(jnp.stack([col_warped] * lax.axis_size("row")), "row", 0, 0), axis=2
+        ),
         preferred_element_type=jnp.float32,
     ).astype(jnp.bfloat16)
     padded = extended(warped, (("row", 2),), reach)

time: 495 us -> 449 us (0.907)
  matrix products: 143 us -> 105 us
  between operations: 14.4 us -> 0.98 us
  starting transfers between devices: 22.4 us -> 32 us
  waiting for transfers between devices: 211 us -> 205 us
    all_gather x1 -> x0, waiting for transfers between devices: 62.1 us -> none  [per_device(): lax.all_gather(col_warped, 'row', axis=2, tiled=True)]
    all_to_all x0 -> x1, waiting for transfers between devices: none -> 56.6 us  [per_device(): lax.all_to_all(jnp.stack([col_warped] * lax.axis_size('row')), 'row', 0, 0)]
    dot_general x18, matrix products: 44.7 us -> 25.3 us  [match_image(): jnp.einsum('kbr,krs->bs', row_table, conv_cols, preferred_element_type=jn...]
    dot_general x19, matrix products: 22.1 us -> 7.15 us  [toeplitz_table(): jnp.einsum('oij,kj->koi', picks, values.astype(jnp.float32))]
    all_to_all x0 -> x1, starting transfers between devices: none -> 5.19 us  [per_device(): lax.all_to_all(jnp.stack([col_warped] * lax.axis_size('row')), 'row', 0, 0)]
where the time goes in v1:
time: 449 us; the launch traced here: 446 us
  waiting for transfers between devices  205 us (46%)
  matrix products  105 us (23%)
  local copies, waits for them, and re-layouts  96.2 us (21%)
  starting transfers between devices  32 us (7%)
  other arithmetic  5.93 us (1%)
    all_to_all x1, waiting for transfers between devices, per_device(): lax.all_to_all(returned, 'det', split_axis=0, concat_axis=0, tiled=True)  72.7 us
    all_to_all x1, waiting for transfers between devices, per_device(): lax.all_to_all(outgoing, 'det', split_axis=0, concat_axis=0, tiled=True)  71 us
    dot_general x18, matrix products, match_image(): jnp.einsum('rtw,kcw->krtc', windows, col_table, preferred_element_type=jn...  57.4 us
    all_to_all x1, waiting for transfers between devices, per_device(): lax.all_to_all(jnp.stack([col_warped] * lax.axis_size('row')), 'row', 0, 0)  56.6 us
    convert_element_type x18, local copies, waits for them, and re-layouts, match_image(): conv_cols = jnp.einsum('rtw,kcw->krtc', windows, col_table, preferred_ele...  54.3 us
    dot_general x18, matrix products, match_image(): jnp.einsum('kbr,krs->bs', row_table, conv_cols, preferred_element_type=jn...  25.3 us
    dynamic_slice x36, local copies, waits for them, and re-layouts, per_device(): matched = lax.map(match_image, (tiles_in, coef_rows))  18.5 us
    all_to_all x1, starting transfers between devices, per_device(): lax.all_to_all(outgoing, 'det', split_axis=0, concat_axis=0, tiled=True)  16.8 us
  transfers between devices with their start and end apart: 5, of which 5 were waited for; matrix products, arithmetic and copies ran while one was open for 1% of the time, Pallas kernels for 0%

profile of v1, /device:TPU:1, one launch (start us, length us, event | category | flops | bytes accessed | tf_op | source)
XLA Modules:
  0.0 445.6 jit_solution(15203651483676817325)
XLA Ops:
  2.0 3.6 convolution_convert_fusion.3
  8.6 5.2 %all-to-all-start = ((bf16[4,6,3,96,384]{4,3,2,1,0:T(8,128)(2,1)}), bf16[4,6,3,96,384]{4,3,2,1,0:T(8,128)(2,1)}, u32[]{:S(2)}, u32[]{:S(2)}) async-start(bf16[4,6,3,96,384]{4,3,2,1,0:T(8,128)(2,1)} %stack.31), calls=%async_computation | async-start | bytes 10616832 | tf_op jit(solution)/shard_map/all_to_all | solution.py:60
  16.3 56.6 %all-to-all-done = bf16[4,6,3,96,384]{4,3,2,1,0:T(8,128)(2,1)} async-done(((bf16[4,6,3,96,384]{4,3,2,1,0:T(8,128)(2,1)}), bf16[4,6,3,96,384]{4,3,2,1,0:T(8,128)(2,1)}, u32[]{:S(2)}, u32[]{:S(2)}) %all-to-all-start) | async-done | bytes 5308448 | tf_op jit(solution)/shard_map/all_to_all | solution.py:60
  72.9 3.5 copy.64
  82.9 3.8 collective-permute-done.1
  88.5 164.2 %while.12 = (s32[]{:T(128)}, f32[18,96,384]{2,1,0:T(8,128)}, f32[18,21]{1,0:T(8,128)S(1)}, f32[21,21]{1,0:T(8,128)S(1)}, bf16[18,116,384]{2,1,0:T(8,128)(2,1)}, /*index=5*/bf16[21,128,148]{1,2,0:T(8,128)(2,1)}, s32[]{:T(128)}) while((s32[]{:T(128)}, f32[18,96,384]{2,1,0:T(8,128)}, f32[18,21]{1,0:T(8,128)S(1)}, f32[21,21]{1,0:T(8,128)S(1)}, ...), condition=%wide.region_1.2_spmd, body=%wide.region_0.1_spmd.sunk | while | flops 468033056 | bytes 10153205 | solution.py:90
  89.6 3.2 convert_bitcast_fusion.2
  92.8 3.0 copy.112
  98.7 3.2 convert_bitcast_fusion.2
  107.8 3.2 convert_bitcast_fusion.2
  117.0 3.2 convert_bitcast_fusion.2
  126.1 3.2 convert_bitcast_fusion.2
  135.2 3.2 convert_bitcast_fusion.2
  144.3 3.2 convert_bitcast_fusion.2
  153.5 3.2 convert_bitcast_fusion.2
  162.6 3.2 convert_bitcast_fusion.2
  171.7 3.2 convert_bitcast_fusion.2
  180.8 3.2 convert_bitcast_fusion.2
  189.9 3.2 convert_bitcast_fusion.2
  199.0 3.2 convert_bitcast_fusion.2
  208.2 3.2 convert_bitcast_fusion.2
  217.3 3.2 convert_bitcast_fusion.2
  226.4 3.2 convert_bitcast_fusion.2
  235.6 3.2 convert_bitcast_fusion.2
  244.7 3.2 convert_bitcast_fusion.2
  257.1 3.7 copy.74
  260.8 16.8 %all-to-all-start.1 = ((bf16[128,96,128]{2,1,0:T(8,128)(2,1)}), bf16[128,96,128]{2,1,0:T(8,128)(2,1)}, u32[]{:S(2)}, u32[]{:S(2)}) async-start(bf16[128,96,128]{2,1,0:T(8,128)(2,1)} %copy.74), calls=%async_computation.1 | async-start | bytes 6291456 | tf_op jit(solution)/shard_map/all_to_all | solution.py:139
  280.1 71.0 %all-to-all-done.1 = bf16[128,96,128]{2,1,0:T(8,128)(2,1)} async-done(((bf16[128,96,128]{2,1,0:T(8,128)(2,1)}), bf16[128,96,128]{2,1,0:T(8,128)(2,1)}, u32[]{:S(2)}, u32[]{:S(2)}) %all-to-all-start.1) | async-done | bytes 3145760 | tf_op jit(solution)/shard_map/all_to_all | solution.py:139
  355.0 3.7 copy.77
  358.7 6.2 %all-to-all-start.2 = ((bf16[128,96,128]{2,1,0:T(8,128)(2,1)}), bf16[128,96,128]{2,1,0:T(8,128)(2,1)}, u32[]{:S(2)}, u32[]{:S(2)}) async-start(bf16[128,96,128]{2,1,0:T(8,128)(2,1)} %copy.77), calls=%async_computation.2 | async-start | bytes 6291456 | tf_op jit(solution)/shard_map/all_to_all | solution.py:148
  365.6 72.7 %all-to-all-done.2 = bf16[128,96,128]{2,1,0:T(8,128)(2,1)} async-done(((bf16[128,96,128]{2,1,0:T(8,128)(2,1)}), bf16[128,96,128]{2,1,0:T(8,128)(2,1)}, u32[]{:S(2)}, u32[]{:S(2)}) %all-to-all-start.2) | async-done | bytes 3145760 | tf_op jit(solution)/shard_map/all_to_all | solution.py:148
  438.4 3.3 fusion.15
  (210 shorter events, 133.0 us)
Async XLA Ops:
  0.6 1.3 copy-start
  8.6 5.3 %copy-start.8 = (s32[384,3]{0,1:T(4,128)S(1)}, s32[384,3]{0,1:T(4,128)}, u32[]{:S(2)}) copy-start(s32[384,3]{0,1:T(4,128)} %param.19) | copy-start | bytes 13828
  8.6 5.3 %copy-start.10 = (f32[8]{0:T(128)S(1)}, f32[8]{0:T(128)}, u32[]{:S(2)}) copy-start(f32[8]{0:T(128)} %param.20) | copy-start | bytes 100
  8.6 5.6 %copy-start.4 = (f32[21,21]{1,0:T(8,128)S(1)}, f32[21,21]{1,0:T(8,128)}, u32[]{:S(2)}) copy-start(f32[21,21]{1,0:T(8,128)} %param.16) | copy-start | bytes 5296
  8.6 64.3 %all-to-all-start = ((bf16[4,6,3,96,384]{4,3,2,1,0:T(8,128)(2,1)}), bf16[4,6,3,96,384]{4,3,2,1,0:T(8,128)(2,1)}, u32[]{:S(2)}, u32[]{:S(2)}) async-start(bf16[4,6,3,96,384]{4,3,2,1,0:T(8,128)(2,1)} %stack.31), calls=%async_computation | async-start | bytes 10616832 | tf_op jit(solution)/shard_map/all_to_all | solution.py:60
  13.8 2.0 copy-start.7
  13.8 2.0 copy-start.6
  13.8 2.0 copy-start.9
  72.9 3.5 copy-start.3
  77.6 5.3 %collective-permute-start = (bf16[6,3,10,384]{3,2,1,0:T(8,128)(2,1)S(1)}, bf16[6,3,10,384]{3,2,1,0:T(8,128)(2,1)S(1)}, u32[]{:S(2)}, u32[]{:S(2)}) collective-permute-start(bf16[6,3,10,384]{3,2,1,0:T(8,128)(2,1)S(1)} %get-tuple-element.125), channel_id=1, source_target_pairs={{0,1},{1,2},{2,3},{4,5},{5,6},{6,7},{8,9},{9,10},{10,11},{12,13},{... | collective-permute-start | bytes 414728 | tf_op jit(solution)/shard_map/ppermute | solution.py:16
  80.0 6.7 %collective-permute-start.1 = (bf16[6,3,10,384]{3,2,1,0:T(8,128)(2,1)S(1)}, bf16[6,3,10,384]{3,2,1,0:T(8,128)(2,1)S(1)}, u32[]{:S(2)}, u32[]{:S(2)}) collective-permute-start(bf16[6,3,10,384]{3,2,1,0:T(8,128)(2,1)S(1)} %get-tuple-element.126), channel_id=1, source_target_pairs={{1,0},{2,1},{3,2},{5,4},{6,5},{7,6},{9,8},{10,9},{11,10},{13,12},{... | collective-permute-start | bytes 414728 | tf_op jit(solution)/shard_map/ppermute | solution.py:17
  260.8 18.0 %copy-start.5 = (s32[3456]{0:T(1024)S(1)}, s32[3456]{0:T(1024)}, u32[]{:S(2)}) copy-start(s32[3456]{0:T(1024)} %param.18) | copy-start | bytes 41476
  260.8 90.3 %all-to-all-start.1 = ((bf16[128,96,128]{2,1,0:T(8,128)(2,1)}), bf16[128,96,128]{2,1,0:T(8,128)(2,1)}, u32[]{:S(2)}, u32[]{:S(2)}) async-start(bf16[128,96,128]{2,1,0:T(8,128)(2,1)} %copy.74), calls=%async_computation.1 | async-start | bytes 6291456 | tf_op jit(solution)/shard_map/all_to_all | solution.py:139
  358.7 79.7 %all-to-all-start.2 = ((bf16[128,96,128]{2,1,0:T(8,128)(2,1)}), bf16[128,96,128]{2,1,0:T(8,128)(2,1)}, u32[]{:S(2)}, u32[]{:S(2)}) async-start(bf16[128,96,128]{2,1,0:T(8,128)(2,1)} %copy.77), calls=%async_computation.2 | async-start | bytes 6291456 | tf_op jit(solution)/shard_map/all_to_all | solution.py:148
  438.4 3.3 copy-start.2
  441.7 3.9 copy-start.1
